TPU v7x, 32 devices: a whole 2x2x4 slice. The times are simulated.
32 devices in a mesh: dp: 4 (over y, x), expert: 8 (over z, core).
Axes of the slice: x: 2, y: 2, z: 4, core: 2. Of those that a mesh axis runs over, the one named last changes fastest.
Arguments:
- out_grad: bfloat16 [4096, 2048], P(('dp', 'expert')), may hold values from -1.1953125 to 1.1953125
- saved_hidden: bfloat16 [4096, 8, 384], P(('dp', 'expert')), may hold values from -6 to 6
- gate_weight: bfloat16 [4096, 8], P(('dp', 'expert')), may hold values from 0.19921875 to 1
- expert_ids: int32 [4096, 8], P(('dp', 'expert')), may hold values from 0 to 31, all different within a row; in each aligned block of 128 rows (0 to 127, 128 to 255, ...) at most 48 rows name the same one
- down_weight: bfloat16 [2048, 32, 384], P('dp', 'expert'), may hold values from -0.3125 to 0.3125
Outputs:
- grad_hidden: bfloat16 [4096, 8, 384], P(('dp', 'expert'))
- grad_gate: bfloat16 [4096, 8], P(('dp', 'expert'))
- grad_down: float32 [2048, 32, 384], P('dp', 'expert')
Inputs may be any that keep to these rules, and one draw needn't show every extreme that they name: `expert_ids`: each token names 8 different experts. Among the tokens of one device no expert is named by more than 48 tokens, and in every draw some expert is named by exactly 48 tokens of some device.
All inputs are finite; a program needn't handle non-finite values.
Results may differ from a plain program's by a relative error of at most 0.014.
Values may be sent and summed in bfloat16 or wider, within the bound.
A program may use at most 128 MiB of HBM per device.

v0:
```python
import jax
import jax.numpy as jnp
from jax import lax
from jax.sharding import PartitionSpec as P


def per_device(out_grad, saved_hidden, gate_weight, expert_ids, down_weight):
    tok_count = out_grad.shape[0]
    top_count = expert_ids.shape[1]
    width = out_grad.shape[1]
    hidden_width = saved_hidden.shape[2]
    owners = lax.axis_size("expert")
    local_experts = down_weight.shape[1]
    total_experts = local_experts * owners
    capacity = max(2, 3 * tok_count * top_count // (2 * total_experts))
    route_count = tok_count * top_count
    slot_count = total_experts * capacity
    flat_ids = expert_ids.reshape(route_count)
    one_hot = (flat_ids[:, None] == jnp.arange(total_experts, dtype=jnp.int32)[None, :]).astype(
        jnp.int32
    )
    before = jnp.cumsum(one_hot, axis=0) - one_hot
    position = jnp.sum(before * one_hot, axis=1)
    slot_of_route = flat_ids * capacity + position
    route_of_slot = (
        jnp.full((slot_count,), route_count, jnp.int32)
        .at[slot_of_route]
        .set(jnp.arange(route_count, dtype=jnp.int32))
    )
    token_of_slot = jnp.where(route_of_slot < route_count, route_of_slot // top_count, tok_count)
    grad_rows = jnp.concatenate([out_grad, jnp.zeros((1, width), out_grad.dtype)], axis=0)[
        token_of_slot
    ]
    hidden_rows = jnp.concatenate(
        [
            saved_hidden.reshape(route_count, hidden_width),
            jnp.zeros((1, hidden_width), saved_hidden.dtype),
        ],
        axis=0,
    )[route_of_slot]
    gate_rows = jnp.concatenate(
        [gate_weight.reshape(route_count), jnp.zeros((1,), gate_weight.dtype)], axis=0
    )[route_of_slot]
    grad_in, hidden_in, gate_in = (
        lax.all_to_all(grad_rows, "expert", split_axis=0, concat_axis=0, tiled=True),
        lax.all_to_all(hidden_rows, "expert", split_axis=0, concat_axis=0, tiled=True),
        lax.all_to_all(gate_rows, "expert", split_axis=0, concat_axis=0, tiled=True),
    )
    grid = (owners, local_experts, capacity)
    grad_in = grad_in.reshape(grid + (width,))
    hidden_in = hidden_in.reshape(grid + (hidden_width,))
    gate_in = gate_in.reshape(grid)
    scaled = (grad_in.astype(jnp.float32) * gate_in.astype(jnp.float32)[..., None]).astype(
        jnp.bfloat16
    )
    full_weight = lax.all_gather(down_weight, "dp", axis=0, tiled=True)
    scaled_part = scaled
    hidden_acc = jnp.einsum(
        "secd,def->secf", scaled_part, full_weight, preferred_element_type=jnp.float32
    )
    recomputed = jnp.einsum(
        "secf,def->secd", hidden_in, full_weight, preferred_element_type=jnp.float32
    )
    gate_acc = jnp.sum(grad_in.astype(jnp.float32) * recomputed, axis=3)
    scaled_part = scaled
    grad_down = lax.psum_scatter(
        jnp.einsum(
            "secd,secf->def", scaled_part, hidden_in, preferred_element_type=jnp.float32
        ).astype(jnp.bfloat16),
        "dp",
        scatter_dimension=0,
        tiled=True,
    ).astype(jnp.float32)
    back_hidden, back_gate = (
        lax.all_to_all(
            hidden_acc.astype(jnp.bfloat16).reshape(slot_count, hidden_width),
            "expert",
            split_axis=0,
            concat_axis=0,
            tiled=True,
        ),
        lax.all_to_all(
            gate_acc.astype(jnp.bfloat16).reshape(slot_count),
            "expert",
            split_axis=0,
            concat_axis=0,
            tiled=True,
        ),
    )
    grad_hidden = back_hidden[slot_of_route].reshape(tok_count, top_count, hidden_width)
    grad_gate = back_gate[slot_of_route].reshape(tok_count, top_count)
    return (grad_hidden, grad_gate, grad_down)


def solution(mesh):
    in_specs = (
        P(("dp", "expert"), None),
        P(("dp", "expert"), None, None),
        P(("dp", "expert"), None),
        P(("dp", "expert"), None),
        P("dp", "expert", None),
    )
    out_specs = (
        P(("dp", "expert"), None, None),
        P(("dp", "expert"), None),
        P("dp", "expert", None),
    )
    return jax.shard_map(
        per_device, mesh=mesh, in_specs=in_specs, out_specs=out_specs, check_vma=False
    )
```

profile of v0, /device:TPU:0, one launch (start us, length us, event | category | flops | bytes accessed | tf_op | source)
XLA Modules:
  0.0 313.0 jit_solution(17395364877933929451)
XLA Ops:
  7.2 0.9 copy.40
  8.9 9.0 %reduce-window.6 = s32[32,8,128]{2,1,0:T(8,128)S(1)} reduce-window(s32[32,8,128]{2,1,0:T(8,128)S(1)} %fusion.23, s32[]{:T(128)} %constant.17.clone.1), window={size=1x1x128 pad=0_0x0_0x127_0}, to_apply=%region_0.0 | reduce-window | flops 4161536 | bytes 262148 | tf_op jit(solution)/shard_map/reduce-window
  18.7 4.3 %scatter_custom_fusion = s32[1536]{0:T(1024)S(1)} fusion(s32[1024]{0:T(1024)S(1)} %bitcast.65, s32[1024]{0:T(1024)S(1)} %iota.11, s32[]{:T(128)} %constant.11.clone.1), kind=kCustom, calls=%fused_computation.42 | custom fusion | bytes 6148 | tf_op jit(solution)/shard_map/scatter | solution.py:28
  23.0 0.8 copy.44
  23.9 9.5 %gather_fusion.1 = bf16[1536]{0:T(1024)(128)(2,1)S(1)} fusion(bf16[1025]{0:T(1024)(128)(2,1)S(1)} %pad_maximum_fusion, s32[2048]{0:T(1024)S(1)} %get-tuple-element.17), kind=kCustom, calls=%fused_computation.1 | custom fusion | bytes 12288 | tf_op jit(solution)/shard_map/gather | solution.py:41
  34.1 6.4 %all-to-all-start.1 = ((bf16[8,192,1]{1,2,0:T(2,128)(2,1)}), bf16[8,192,1]{1,2,0:T(2,128)(2,1)S(1)}, u32[]{:S(2)}, u32[]{:S(2)}) async-start(bf16[8,192,1]{1,2,0:T(2,128)(2,1)} %all_to_all.43), calls=%async_computation.1 | async-start | bytes 16384 | tf_op jit(solution)/shard_map/all_to_all | solution.py:47
  40.6 5.3 %gather_fusion.3 = bf16[1536,384]{1,0:T(8,128)(2,1)} fusion(bf16[1025,384]{1,0:T(8,128)(2,1)S(1)} %concatenate.11, s32[2048]{0:T(1024)S(1)} %get-tuple-element.17), kind=kCustom, calls=%fused_computation.3 | custom fusion | bytes 2365440 | tf_op jit(solution)/shard_map/gather | solution.py:34
  46.1 4.9 %all-to-all-start.3 = ((bf16[8,192,384]{2,1,0:T(8,128)(2,1)}), bf16[8,192,384]{2,1,0:T(8,128)(2,1)S(1)}, u32[]{:S(2)}, u32[]{:S(2)}) async-start(bf16[8,192,384]{2,1,0:T(8,128)(2,1)} %bitcast.14), calls=%async_computation.3 | async-start | bytes 2359296 | tf_op jit(solution)/shard_map/all_to_all | solution.py:46
  51.0 7.1 %gather_fusion = bf16[1536,2048]{1,0:T(8,128)(2,1)} fusion(bf16[129,2048]{1,0:T(8,128)(2,1)S(1)} %concatenate.9, s32[2048]{0:T(1024)S(1)} %get-tuple-element.18), kind=kCustom, calls=%fused_computation | custom fusion | bytes 12589056 | tf_op jit(solution)/shard_map/gather | solution.py:31
  58.2 22.2 %all-to-all-done.3 = bf16[8,192,384]{2,1,0:T(8,128)(2,1)S(1)} async-done(((bf16[8,192,384]{2,1,0:T(8,128)(2,1)}), bf16[8,192,384]{2,1,0:T(8,128)(2,1)S(1)}, u32[]{:S(2)}, u32[]{:S(2)}) %all-to-all-start.3) | async-done | bytes 1179680 | tf_op jit(solution)/shard_map/all_to_all | solution.py:46
  80.3 4.9 %all-to-all-start = ((bf16[8,192,2048]{2,1,0:T(8,128)(2,1)}), bf16[8,192,2048]{2,1,0:T(8,128)(2,1)}, u32[]{:S(2)}, u32[]{:S(2)}) async-start(bf16[8,192,2048]{2,1,0:T(8,128)(2,1)} %bitcast.57), calls=%async_computation | async-start | bytes 12582912 | tf_op jit(solution)/shard_map/all_to_all | solution.py:45
  85.3 1.3 copy.46
  86.8 137.3 %all-to-all-done = bf16[8,192,2048]{2,1,0:T(8,128)(2,1)} async-done(((bf16[8,192,2048]{2,1,0:T(8,128)(2,1)}), bf16[8,192,2048]{2,1,0:T(8,128)(2,1)}, u32[]{:S(2)}, u32[]{:S(2)}) %all-to-all-start) | async-done | bytes 6291488 | tf_op jit(solution)/shard_map/all_to_all | solution.py:45
  224.1 9.0 %fusion.1 = bf16[2048,4,384]{0,2,1:T(8,128)(2,1)} fusion(bf16[8,4,48,384]{3,2,1,0:T(8,128)(2,1)S(1)} %bitcast.58, f32[8,4,48]{2,1,0:T(4,128)S(1)} %reshape.113, bf16[8,4,48,2048]{3,2,1,0:T(8,128)(2,1)} %bitcast.12), kind=kOutput, calls=%fused_computation.10 | convolution fusion | flops 2428502016 | bytes 13768704 | tf_op jit(solution)/shard_map/secd,secf->def/dot_general | solution.py:67
  233.2 8.7 %fusion = bf16[8,4,48]{2,0,1:T(8,128)(2,1)S(1)} fusion(bf16[2048,4,384]{2,0,1:T(8,128)(2,1)} %all-gather.2.cloned.1.call-done, bf16[8,4,48,384]{3,2,1,0:T(8,128)(2,1)S(1)} %bitcast.59, bf16[8,4,48,2048]{3,2,1,0:T(8,128)(2,1)} %bitcast.12), kind=kOutput, calls=%fused_computation.8 | convolution fusion | flops 2425354752 | bytes 13765632 | tf_op jit(solution)/shard_map/secf,def->secd/dot_general | solution.py:61
  242.6 3.5 %all-to-all-start.4 = ((bf16[8,192,1]{1,2,0:T(2,128)(2,1)}), bf16[8,192,1]{1,2,0:T(2,128)(2,1)S(1)}, u32[]{:S(2)}, u32[]{:S(2)}) async-start(bf16[8,192,1]{1,2,0:T(2,128)(2,1)} %convert_element_type.72), calls=%async_computation.4 | async-start | bytes 16384 | tf_op jit(solution)/shard_map/all_to_all | solution.py:82
  246.1 8.4 %fusion.14 = bf16[8,4,48,384]{3,2,0,1:T(8,128)(2,1)S(1)} fusion(bf16[2048,4,384]{2,0,1:T(8,128)(2,1)} %all-gather.2.cloned.1.call-done, f32[8,4,48]{2,1,0:T(4,128)S(1)} %reshape.113, bf16[8,4,48,2048]{3,2,1,0:T(8,128)(2,1)} %bitcast.12), kind=kOutput, calls=%fused_computation.17 | convolution fusion | flops 2425946112 | bytes 13768704 | tf_op jit(solution)/shard_map/secd,def->secf/dot_general | solution.py:58
  254.6 1.1 copy.48
  255.7 4.8 %all-to-all-start.2 = ((bf16[8,192,384]{2,1,0:T(8,128)(2,1)}), bf16[8,192,384]{2,1,0:T(8,128)(2,1)S(1)}, u32[]{:S(2)}, u32[]{:S(2)}) async-start(bf16[8,192,384]{2,1,0:T(8,128)(2,1)} %bitcast.9), calls=%async_computation.2 | async-start | bytes 2359296 | tf_op jit(solution)/shard_map/all_to_all | solution.py:75
  260.6 6.8 %gather_fusion.4 = bf16[1024]{0:T(1024)(128)(2,1)S(1)} fusion(bf16[1536]{0:T(1024)(128)(2,1)S(1)} %all_to_all.42, s32[1024]{0:T(1024)S(1)} %broadcast_clamp_fusion), kind=kCustom, calls=%fused_computation.4 | custom fusion | bytes 8192 | tf_op jit(solution)/shard_map/gather | solution.py:91
  268.2 21.7 %all-to-all-done.2 = bf16[8,192,384]{2,1,0:T(8,128)(2,1)S(1)} async-done(((bf16[8,192,384]{2,1,0:T(8,128)(2,1)}), bf16[8,192,384]{2,1,0:T(8,128)(2,1)S(1)}, u32[]{:S(2)}, u32[]{:S(2)}) %all-to-all-start.2) | async-done | bytes 1179680 | tf_op jit(solution)/shard_map/all_to_all | solution.py:75
  289.9 5.0 %gather_fusion.2 = bf16[1024,384]{1,0:T(8,128)(2,1)} fusion(bf16[1536,384]{1,0:T(8,128)(2,1)S(1)} %bitcast.56, s32[1024]{0:T(1024)S(1)} %broadcast_clamp_fusion), kind=kCustom, calls=%fused_computation.2 | custom fusion | bytes 1576960 | tf_op jit(solution)/shard_map/gather | solution.py:90
  294.9 7.4 %reduce-scatter.2.cloned.1.call-done = bf16[512,4,384]{0,2,1:T(8,128)(2,1)} async-done(((bf16[2048,4,384]{0,2,1:T(8,128)(2,1)}), bf16[512,4,384]{0,2,1:T(8,128)(2,1)}) %reduce-scatter.2.cloned.1.call-update) | async-done | bytes 1572880 | tf_op jit(solution)/shard_map/reduce_scatter | solution.py:66
  302.3 3.9 %copy.54 = f32[512,4,384]{2,1,0:T(4,128)} copy(bf16[512,4,384]{0,2,1:T(8,128)(2,1)} %reduce-scatter.2.cloned.1.call-done) | data formatting | bytes 4718592
  (44 shorter events, 4.5 us)
Async XLA Ops:
  7.2 33.3 %copy-start.1 = (bf16[128,8,384]{2,1,0:T(8,128)(2,1)S(1)}, bf16[128,8,384]{2,1,0:T(8,128)(2,1)}, u32[]{:S(2)}) copy-start(bf16[128,8,384]{2,1,0:T(8,128)(2,1)} %param.6) | copy-start | bytes 2359300
  34.1 12.0 %all-to-all-start.1 = ((bf16[8,192,1]{1,2,0:T(2,128)(2,1)}), bf16[8,192,1]{1,2,0:T(2,128)(2,1)S(1)}, u32[]{:S(2)}, u32[]{:S(2)}) async-start(bf16[8,192,1]{1,2,0:T(2,128)(2,1)} %all_to_all.43), calls=%async_computation.1 | async-start | bytes 16384 | tf_op jit(solution)/shard_map/all_to_all | solution.py:47
  40.5 10.4 %copy-start.2 = (bf16[128,2048]{1,0:T(8,128)(2,1)S(1)}, bf16[128,2048]{1,0:T(8,128)(2,1)}, u32[]{:S(2)}) copy-start(bf16[128,2048]{1,0:T(8,128)(2,1)} %param.5) | copy-start | bytes 1572868
  46.1 34.3 %all-to-all-start.3 = ((bf16[8,192,384]{2,1,0:T(8,128)(2,1)}), bf16[8,192,384]{2,1,0:T(8,128)(2,1)S(1)}, u32[]{:S(2)}, u32[]{:S(2)}) async-start(bf16[8,192,384]{2,1,0:T(8,128)(2,1)} %bitcast.14), calls=%async_computation.3 | async-start | bytes 2359296 | tf_op jit(solution)/shard_map/all_to_all | solution.py:46
  80.3 4.9 %copy-start = (bf16[512,4,384]{2,1,0:T(4,128)(2,1)S(1)}, bf16[512,4,384]{2,1,0:T(4,128)(2,1)}, u32[]{:S(2)}) copy-start(bf16[512,4,384]{2,1,0:T(4,128)(2,1)} %param.9) | copy-start | bytes 4718596
  80.3 143.8 %all-to-all-start = ((bf16[8,192,2048]{2,1,0:T(8,128)(2,1)}), bf16[8,192,2048]{2,1,0:T(8,128)(2,1)}, u32[]{:S(2)}, u32[]{:S(2)}) async-start(bf16[8,192,2048]{2,1,0:T(8,128)(2,1)} %bitcast.57), calls=%async_computation | async-start | bytes 12582912 | tf_op jit(solution)/shard_map/all_to_all | solution.py:45
  85.2 148.0 %all-gather.2.cloned.1.call-start = ((), (), s32[]{:S(2)}) async-start(), calls=%async_computation.6 | async-start | bytes 7864320 | tf_op jit(solution)/shard_map/all_gather | solution.py:56
  86.6 215.6 %reduce-scatter.2.cloned.1.call-start = ((), (), s32[]{:S(2)}) async-start(), calls=%async_computation.7 | async-start | bytes 7864320 | tf_op jit(solution)/shard_map/reduce_scatter | solution.py:66
  242.6 13.1 %all-to-all-start.4 = ((bf16[8,192,1]{1,2,0:T(2,128)(2,1)}), bf16[8,192,1]{1,2,0:T(2,128)(2,1)S(1)}, u32[]{:S(2)}, u32[]{:S(2)}) async-start(bf16[8,192,1]{1,2,0:T(2,128)(2,1)} %convert_element_type.72), calls=%async_computation.4 | async-start | bytes 16384 | tf_op jit(solution)/shard_map/all_to_all | solution.py:82
  255.7 34.1 %all-to-all-start.2 = ((bf16[8,192,384]{2,1,0:T(8,128)(2,1)}), bf16[8,192,384]{2,1,0:T(8,128)(2,1)S(1)}, u32[]{:S(2)}, u32[]{:S(2)}) async-start(bf16[8,192,384]{2,1,0:T(8,128)(2,1)} %bitcast.9), calls=%async_computation.2 | async-start | bytes 2359296 | tf_op jit(solution)/shard_map/all_to_all | solution.py:75
Sparse Core Ops, SparseCore 0:
  88.4 71.3 all-gather.1
  233.3 68.9 reduce-scatter.1
where the time goes:
time: 314 us; the launch traced here: 313 us
  waiting for transfers between devices  189 us (60%)
  local copies, waits for them, and re-layouts  49.3 us (16%)
  matrix products  26.2 us (8%)
  starting transfers between devices  24.5 us (8%)
  between operations  14.2 us (5%)
  other arithmetic  9.99 us (3%)
    all_to_all x1, waiting for transfers between devices, per_device(): lax.all_to_all(grad_rows, 'expert', split_axis=0, concat_axis=0, tiled=True)  137 us
    all_to_all x1, waiting for transfers between devices, per_device(): lax.all_to_all(hidden_rows, 'expert', split_axis=0, concat_axis=0, tiled=...  22.2 us
    all_to_all x1, waiting for transfers between devices, per_device(): lax.all_to_all(hidden_acc.astype(jnp.bfloat16).reshape(slot_count, hidden...  21.7 us
    gather x1, local copies, waits for them, and re-layouts, per_device(): jnp.concatenate([gate_weight.reshape(route_count), jnp.zeros((1,), gate_w...  9.46 us
    another operation x3, other arithmetic  9.15 us
    dot_general x1, matrix products, per_device(): jnp.einsum('secd,secf->def', scaled_part, hidden_in, preferred_element_ty...  9 us
    dot_general x1, matrix products, per_device(): jnp.einsum('secf,def->secd', hidden_in, full_weight, preferred_element_ty...  8.74 us
    dot_general x1, matrix products, per_device(): jnp.einsum('secd,def->secf', scaled_part, full_weight, preferred_element_...  8.41 us
  transfers between devices with their start and end apart: 7, of which 5 were waited for; matrix products, arithmetic and copies ran while one was open for 17% of the time, Pallas kernels for 0%

commit v1 on v0

--- a/solution.py
+++ b/solution.py
@@ -1,7 +1,38 @@
+import functools
 import jax
 import jax.numpy as jnp
 from jax import lax
 from jax.sharding import PartitionSpec as P
+
+
+def _direct_plate(mat, dim_at, q_in):
+    n_now, item_now = (mat.shape[:dim_at], mat.shape[dim_at + 1 :])
+    part_now = mat.reshape(*n_now, q_in, -1, *item_now)
+    return jnp.moveaxis(part_now, dim_at, 0)
+
+
+def load_ratios(w_in, join_dim):
+    f_next = list(w_in.shape[1:])
+    f_next[join_dim] *= w_in.shape[0]
+    return jnp.moveaxis(w_in, 0, join_dim).reshape(f_next)
+
+
+def post_sheets(v0, mesh_name, inner_x, content):
+    taken_in = lax.axis_size(mesh_name)
+    arr_next = lax.axis_index(mesh_name)
+    near, r2 = (taken_in, arr_next)
+    shaped = _direct_plate(v0, inner_x, near)
+    placed = shaped
+    for it in range(1, near):
+        last, earlier = ((r2 + it) % near, (r2 - it) % near)
+        top = lax.dynamic_index_in_dim(shaped, last, 0)
+        vec_out = tuple(((u, (u + it) % near) for u in range(near)))
+        small = lax.ppermute(top, axis_name=mesh_name, perm=vec_out)
+        placed = lax.dynamic_update_slice_in_dim(placed, small, earlier, axis=0)
+    return load_ratios(placed, content)
+
+
+carry_node = functools.partial(post_sheets, mesh_name="expert", inner_x=0, content=0)
 
 
 def per_device(out_grad, saved_hidden, gate_weight, expert_ids, down_weight):
@@ -72,13 +103,7 @@
         tiled=True,
     ).astype(jnp.float32)
     back_hidden, back_gate = (
-        lax.all_to_all(
-            hidden_acc.astype(jnp.bfloat16).reshape(slot_count, hidden_width),
-            "expert",
-            split_axis=0,
-            concat_axis=0,
-            tiled=True,
-        ),
+        carry_node(hidden_acc.astype(jnp.bfloat16).reshape(slot_count, hidden_width)),
         lax.all_to_all(
             gate_acc.astype(jnp.bfloat16).reshape(slot_count),
             "expert",

time: 314 us -> 314 us (level)
  starting transfers between devices: 24.5 us -> 28.4 us
  matrix products: 26.2 us -> 23 us
    all_to_all x1 -> x0, waiting for transfers between devices: 21.7 us -> none  [per_device(): lax.all_to_all(hidden_acc.astype(jnp.bfloat16).reshape(slot_count, hidden...]
    reduce_scatter x1, waiting for transfers between devices: 7.39 us -> 18.7 us  [per_device(): lax.psum_scatter(jnp.einsum('secd,secf->def', scaled_part, hidden_in, pre...]
    ppermute x0 -> x7, waiting for transfers between devices: none -> 7.65 us  [post_sheets(): small = lax.ppermute(top, axis_name=mesh_name, perm=vec_out)]
    ppermute x0 -> x7, starting transfers between devices: none -> 7.31 us  [post_sheets(): small = lax.ppermute(top, axis_name=mesh_name, perm=vec_out)]
    all_to_all x1 -> x0, starting transfers between devices: 4.78 us -> none  [per_device(): lax.all_to_all(hidden_acc.astype(jnp.bfloat16).reshape(slot_count, hidden...]
    unnamed x11 -> x13, local copies, waits for them, and re-layouts: 7.57 us -> 7.5 us
  transfers between devices with their start and end apart: 7 -> 13, of which waited for: 5 -> 8; matrix products, arithmetic and copies ran while one was open for 17% -> 16% of each run, Pallas kernels for 0% -> 0%
where the time goes in v1:
time: 314 us; the launch traced here: 313 us
  waiting for transfers between devices  189 us (60%)
  local copies, waits for them, and re-layouts  48.5 us (15%)
  starting transfers between devices  28.4 us (9%)
  matrix products  23 us (7%)
  between operations  14.4 us (5%)
  other arithmetic  9.99 us (3%)
    all_to_all x1, waiting for transfers between devices, per_device(): lax.all_to_all(grad_rows, 'expert', split_axis=0, concat_axis=0, tiled=True)  137 us
    all_to_all x1, waiting for transfers between devices, per_device(): lax.all_to_all(hidden_rows, 'expert', split_axis=0, concat_axis=0, tiled=...  22.2 us
    reduce_scatter x1, waiting for transfers between devices, per_device(): lax.psum_scatter(jnp.einsum('secd,secf->def', scaled_part, hidden_in, pre...  18.7 us
    gather x1, local copies, waits for them, and re-layouts, per_device(): jnp.concatenate([gate_weight.reshape(route_count), jnp.zeros((1,), gate_w...  9.46 us
    another operation x3, other arithmetic  9.15 us
    dot_general x1, matrix products, per_device(): jnp.einsum('secd,secf->def', scaled_part, hidden_in, preferred_element_ty...  8.98 us
    dot_general x1, matrix products, per_device(): jnp.einsum('secd,def->secf', scaled_part, full_weight, preferred_element_...  8.2 us
    ppermute x7, waiting for transfers between devices, post_sheets(): small = lax.ppermute(top, axis_name=mesh_name, perm=vec_out)  7.65 us
  transfers between devices with their start and end apart: 13, of which 8 were waited for; matrix products, arithmetic and copies ran while one was open for 16% of the time, Pallas kernels for 0%

profile of v1, /device:TPU:0, one launch (start us, length us, event | category | flops | bytes accessed | tf_op | source)
XLA Modules:
  0.0 313.0 jit_solution(4674375953453696558)
XLA Ops:
  10.0 9.0 %reduce-window.6 = s32[32,8,128]{2,1,0:T(8,128)S(1)} reduce-window(s32[32,8,128]{2,1,0:T(8,128)S(1)} %fusion.23, s32[]{:T(128)} %constant.125.clone.1), window={size=1x1x128 pad=0_0x0_0x127_0}, to_apply=%region_0.0 | reduce-window | flops 4161536 | bytes 262148 | tf_op jit(solution)/shard_map/reduce-window
  19.5 4.3 %scatter_custom_fusion = s32[1536]{0:T(1024)S(1)} fusion(s32[1024]{0:T(1024)S(1)} %bitcast.67, s32[1024]{0:T(1024)S(1)} %iota.11, s32[]{:T(128)} %constant.123.clone.1), kind=kCustom, calls=%fused_computation.42 | custom fusion | bytes 6148 | tf_op jit(solution)/shard_map/scatter | solution.py:59
  23.9 9.5 %gather_fusion.1 = bf16[1536]{0:T(1024)(128)(2,1)S(1)} fusion(bf16[1025]{0:T(1024)(128)(2,1)S(1)} %pad_maximum_fusion, s32[2048]{0:T(1024)S(1)} %get-tuple-element.24), kind=kCustom, calls=%fused_computation.1 | custom fusion | bytes 12288 | tf_op jit(solution)/shard_map/gather | solution.py:72
  34.0 6.4 %all-to-all-start.1 = ((bf16[8,192,1]{1,2,0:T(2,128)(2,1)}), bf16[8,192,1]{1,2,0:T(2,128)(2,1)S(1)}, u32[]{:S(2)}, u32[]{:S(2)}) async-start(bf16[8,192,1]{1,2,0:T(2,128)(2,1)} %all_to_all.32), calls=%async_computation.1 | async-start | bytes 16384 | tf_op jit(solution)/shard_map/all_to_all | solution.py:78
  40.5 5.3 %gather_fusion.3 = bf16[1536,384]{1,0:T(8,128)(2,1)} fusion(bf16[1025,384]{1,0:T(8,128)(2,1)S(1)} %concatenate.11, s32[2048]{0:T(1024)S(1)} %get-tuple-element.24), kind=kCustom, calls=%fused_computation.3 | custom fusion | bytes 2365440 | tf_op jit(solution)/shard_map/gather | solution.py:65
  46.0 5.0 %all-to-all-start.2 = ((bf16[8,192,384]{2,1,0:T(8,128)(2,1)}), bf16[8,192,384]{2,1,0:T(8,128)(2,1)S(1)}, u32[]{:S(2)}, u32[]{:S(2)}) async-start(bf16[8,192,384]{2,1,0:T(8,128)(2,1)} %bitcast.14), calls=%async_computation.2 | async-start | bytes 2359296 | tf_op jit(solution)/shard_map/all_to_all | solution.py:77
  51.1 7.1 %gather_fusion = bf16[1536,2048]{1,0:T(8,128)(2,1)} fusion(bf16[129,2048]{1,0:T(8,128)(2,1)S(1)} %concatenate.9, s32[2048]{0:T(1024)S(1)} %get-tuple-element.25), kind=kCustom, calls=%fused_computation | custom fusion | bytes 12589056 | tf_op jit(solution)/shard_map/gather | solution.py:62
  58.2 22.2 %all-to-all-done.2 = bf16[8,192,384]{2,1,0:T(8,128)(2,1)S(1)} async-done(((bf16[8,192,384]{2,1,0:T(8,128)(2,1)}), bf16[8,192,384]{2,1,0:T(8,128)(2,1)S(1)}, u32[]{:S(2)}, u32[]{:S(2)}) %all-to-all-start.2) | async-done | bytes 1179680 | tf_op jit(solution)/shard_map/all_to_all | solution.py:77
  80.4 4.9 %all-to-all-start = ((bf16[8,192,2048]{2,1,0:T(8,128)(2,1)}), bf16[8,192,2048]{2,1,0:T(8,128)(2,1)}, u32[]{:S(2)}, u32[]{:S(2)}) async-start(bf16[8,192,2048]{2,1,0:T(8,128)(2,1)} %bitcast.59), calls=%async_computation | async-start | bytes 12582912 | tf_op jit(solution)/shard_map/all_to_all | solution.py:76
  85.3 1.3 copy.46
  86.9 137.3 %all-to-all-done = bf16[8,192,2048]{2,1,0:T(8,128)(2,1)} async-done(((bf16[8,192,2048]{2,1,0:T(8,128)(2,1)}), bf16[8,192,2048]{2,1,0:T(8,128)(2,1)}, u32[]{:S(2)}, u32[]{:S(2)}) %all-to-all-start) | async-done | bytes 6291488 | tf_op jit(solution)/shard_map/all_to_all | solution.py:76
  224.2 9.0 %fusion.1 = bf16[2048,4,384]{0,2,1:T(8,128)(2,1)} fusion(bf16[8,4,48,384]{3,2,1,0:T(8,128)(2,1)S(1)} %bitcast.60, f32[8,4,48]{2,1,0:T(4,128)S(1)} %reshape.113, bf16[8,4,48,2048]{3,2,1,0:T(8,128)(2,1)} %bitcast.12), kind=kOutput, calls=%fused_computation.10 | convolution fusion | flops 2428502016 | bytes 13768704 | tf_op jit(solution)/shard_map/secd,secf->def/dot_general | solution.py:98
  233.3 8.2 %fusion.14 = bf16[8,4,48,384]{3,2,0,1:T(8,128)(2,1)S(1)} fusion(bf16[2048,4,384]{2,0,1:T(8,128)(2,1)} %all-gather.2.cloned.1.call-done, f32[8,4,48]{2,1,0:T(4,128)S(1)} %reshape.113, bf16[8,4,48,2048]{3,2,1,0:T(8,128)(2,1)} %bitcast.12), kind=kOutput, calls=%fused_computation.17 | convolution fusion | flops 2425946112 | bytes 13768704 | tf_op jit(solution)/shard_map/secd,def->secf/dot_general | solution.py:89
  242.0 5.8 %fusion = bf16[8,4,48]{2,0,1:T(8,128)(2,1)S(1)} fusion(bf16[2048,4,384]{2,0,1:T(8,128)(2,1)S(1)} %copy-done.3, bf16[8,4,48,384]{3,2,1,0:T(8,128)(2,1)S(1)} %bitcast.61, bf16[8,4,48,2048]{3,2,1,0:T(8,128)(2,1)} %bitcast.12), kind=kOutput, calls=%fused_computation.8 | convolution fusion | flops 2425354752 | bytes 13765632 | tf_op jit(solution)/shard_map/secf,def->secd/dot_general | solution.py:92
  248.5 4.8 %all-to-all-start.3 = ((bf16[8,192,1]{1,2,0:T(2,128)(2,1)}), bf16[8,192,1]{1,2,0:T(2,128)(2,1)S(1)}, u32[]{:S(2)}, u32[]{:S(2)}) async-start(bf16[8,192,1]{1,2,0:T(2,128)(2,1)} %convert_element_type.72), calls=%async_computation.3 | async-start | bytes 16384 | tf_op jit(solution)/shard_map/all_to_all | solution.py:107
  253.5 2.1 collective-permute-start.1
  256.4 2.5 all-to-all-done.3
  259.1 6.8 %gather_fusion.4 = bf16[1024]{0:T(1024)(128)(2,1)S(1)} fusion(bf16[1536]{0:T(1024)(128)(2,1)S(1)} %all_to_all.31, s32[1024]{0:T(1024)S(1)} %broadcast_clamp_fusion), kind=kCustom, calls=%fused_computation.4 | custom fusion | bytes 8192 | tf_op jit(solution)/shard_map/gather | solution.py:116
  267.2 1.5 collective-permute-start.4
  269.6 1.1 collective-permute-start.6
  270.8 7.2 %collective-permute-done.3 = bf16[1,192,384]{2,1,0:T(8,128)(2,1)S(1)} collective-permute-done((bf16[1,192,384]{2,1,0:T(8,128)(2,1)S(1)}, bf16[1,192,384]{2,1,0:T(8,128)(2,1)S(1)}, u32[]{:S(2)}, u32[]{:S(2)}) %collective-permute-start.3) | collective-permute-done | bytes 147488 | tf_op jit(solution)/shard_map/ppermute | solution.py:30
  278.6 5.0 %gather_fusion.2 = bf16[1024,384]{1,0:T(8,128)(2,1)} fusion(bf16[1536,384]{1,0:T(8,128)(2,1)S(1)} %bitcast.58, s32[1024]{0:T(1024)S(1)} %broadcast_clamp_fusion), kind=kCustom, calls=%fused_computation.2 | custom fusion | bytes 1576960 | tf_op jit(solution)/shard_map/gather | solution.py:115
  283.6 18.7 %reduce-scatter.2.cloned.1.call-done = bf16[512,4,384]{0,2,1:T(8,128)(2,1)} async-done(((bf16[2048,4,384]{0,2,1:T(8,128)(2,1)}), bf16[512,4,384]{0,2,1:T(8,128)(2,1)}) %reduce-scatter.2.cloned.1.call-update) | async-done | bytes 1572880 | tf_op jit(solution)/shard_map/reduce_scatter | solution.py:97
  302.3 3.9 %copy.54 = f32[512,4,384]{2,1,0:T(4,128)} copy(bf16[512,4,384]{0,2,1:T(8,128)(2,1)} %reduce-scatter.2.cloned.1.call-done) | data formatting | bytes 4718592
  (66 shorter events, 9.7 us)
Async XLA Ops:
  19.3 21.1 %copy-start.1 = (bf16[128,8,384]{2,1,0:T(8,128)(2,1)S(1)}, bf16[128,8,384]{2,1,0:T(8,128)(2,1)}, u32[]{:S(2)}) copy-start(bf16[128,8,384]{2,1,0:T(8,128)(2,1)} %param.6) | copy-start | bytes 2359300
  34.0 12.0 %all-to-all-start.1 = ((bf16[8,192,1]{1,2,0:T(2,128)(2,1)}), bf16[8,192,1]{1,2,0:T(2,128)(2,1)S(1)}, u32[]{:S(2)}, u32[]{:S(2)}) async-start(bf16[8,192,1]{1,2,0:T(2,128)(2,1)} %all_to_all.32), calls=%async_computation.1 | async-start | bytes 16384 | tf_op jit(solution)/shard_map/all_to_all | solution.py:78
  45.8 5.2 %copy-start.2 = (bf16[128,2048]{1,0:T(8,128)(2,1)S(1)}, bf16[128,2048]{1,0:T(8,128)(2,1)}, u32[]{:S(2)}) copy-start(bf16[128,2048]{1,0:T(8,128)(2,1)} %param.5) | copy-start | bytes 1572868
  46.0 34.4 %all-to-all-start.2 = ((bf16[8,192,384]{2,1,0:T(8,128)(2,1)}), bf16[8,192,384]{2,1,0:T(8,128)(2,1)S(1)}, u32[]{:S(2)}, u32[]{:S(2)}) async-start(bf16[8,192,384]{2,1,0:T(8,128)(2,1)} %bitcast.14), calls=%async_computation.2 | async-start | bytes 2359296 | tf_op jit(solution)/shard_map/all_to_all | solution.py:77
  80.4 5.0 %copy-start = (bf16[512,4,384]{2,1,0:T(4,128)(2,1)S(1)}, bf16[512,4,384]{2,1,0:T(4,128)(2,1)}, u32[]{:S(2)}) copy-start(bf16[512,4,384]{2,1,0:T(4,128)(2,1)} %param.9) | copy-start | bytes 4718596
  80.4 143.8 %all-to-all-start = ((bf16[8,192,2048]{2,1,0:T(8,128)(2,1)}), bf16[8,192,2048]{2,1,0:T(8,128)(2,1)}, u32[]{:S(2)}, u32[]{:S(2)}) async-start(bf16[8,192,2048]{2,1,0:T(8,128)(2,1)} %bitcast.59), calls=%async_computation | async-start | bytes 12582912 | tf_op jit(solution)/shard_map/all_to_all | solution.py:76
  85.3 148.1 %all-gather.2.cloned.1.call-start = ((), (), s32[]{:S(2)}) async-start(), calls=%async_computation.5 | async-start | bytes 7864320 | tf_op jit(solution)/shard_map/all_gather | solution.py:87
  86.7 215.6 %reduce-scatter.2.cloned.1.call-start = ((), (), s32[]{:S(2)}) async-start(), calls=%async_computation.6 | async-start | bytes 7864320 | tf_op jit(solution)/shard_map/reduce_scatter | solution.py:97
  233.3 8.6 %copy-start.3 = (bf16[2048,4,384]{2,0,1:T(8,128)(2,1)S(1)}, bf16[2048,4,384]{2,0,1:T(8,128)(2,1)}, u32[]{:S(2)}) copy-start(bf16[2048,4,384]{2,0,1:T(8,128)(2,1)} %all-gather.2.cloned.1.call-done) | copy-start | bytes 18874372
  241.7 11.6 %collective-permute-start = (bf16[1,192,384]{2,1,0:T(8,128)(2,1)S(1)}, bf16[1,192,384]{2,1,0:T(8,128)(2,1)S(1)}, u32[]{:S(2)}, u32[]{:S(2)}) collective-permute-start(bf16[1,192,384]{2,1,0:T(8,128)(2,1)S(1)} %constant_dynamic-slice_fusion.6), channel_id=1, source_target_pairs={{0,1},{1,2},{2,3},{3,4},{4,5},{5,6},{6,7},{7,0},{8,9},{9,10},{10,1... | collective-permute-start | bytes 442376 | tf_op jit(solution)/shard_map/ppermute | solution.py:30
  248.5 10.4 %all-to-all-start.3 = ((bf16[8,192,1]{1,2,0:T(2,128)(2,1)}), bf16[8,192,1]{1,2,0:T(2,128)(2,1)S(1)}, u32[]{:S(2)}, u32[]{:S(2)}) async-start(bf16[8,192,1]{1,2,0:T(2,128)(2,1)} %convert_element_type.72), calls=%async_computation.3 | async-start | bytes 16384 | tf_op jit(solution)/shard_map/all_to_all | solution.py:107
  253.5 16.2 %collective-permute-start.1 = (bf16[1,192,384]{2,1,0:T(8,128)(2,1)S(1)}, bf16[1,192,384]{2,1,0:T(8,128)(2,1)S(1)}, u32[]{:S(2)}, u32[]{:S(2)}) collective-permute-start(bf16[1,192,384]{2,1,0:T(8,128)(2,1)S(1)} %get-tuple-element.20), channel_id=1, source_target_pairs={{0,2},{1,3},{2,4},{3,5},{4,6},{5,7},{6,0},{7,1},{8,10},{9,11},{10,... | collective-permute-start | bytes 442376 | tf_op jit(solution)/shard_map/ppermute | solution.py:30
  255.5 15.3 %collective-permute-start.2 = (bf16[1,192,384]{2,1,0:T(8,128)(2,1)S(1)}, bf16[1,192,384]{2,1,0:T(8,128)(2,1)S(1)}, u32[]{:S(2)}, u32[]{:S(2)}) collective-permute-start(bf16[1,192,384]{2,1,0:T(8,128)(2,1)S(1)} %get-tuple-element.19), channel_id=1, source_target_pairs={{0,3},{1,4},{2,5},{3,6},{4,7},{5,0},{6,1},{7,2},{8,11},{9,12},{10,... | collective-permute-start | bytes 442376 | tf_op jit(solution)/shard_map/ppermute | solution.py:30
  266.7 11.4 %collective-permute-start.3 = (bf16[1,192,384]{2,1,0:T(8,128)(2,1)S(1)}, bf16[1,192,384]{2,1,0:T(8,128)(2,1)S(1)}, u32[]{:S(2)}, u32[]{:S(2)}) collective-permute-start(bf16[1,192,384]{2,1,0:T(8,128)(2,1)S(1)} %get-tuple-element.18), channel_id=1, source_target_pairs={{0,4},{1,5},{2,6},{3,7},{4,0},{5,1},{6,2},{7,3},{8,12},{9,13},{10,... | collective-permute-start | bytes 442376 | tf_op jit(solution)/shard_map/ppermute | solution.py:30
  267.2 10.9 %collective-permute-start.4 = (bf16[1,192,384]{2,1,0:T(8,128)(2,1)S(1)}, bf16[1,192,384]{2,1,0:T(8,128)(2,1)S(1)}, u32[]{:S(2)}, u32[]{:S(2)}) collective-permute-start(bf16[1,192,384]{2,1,0:T(8,128)(2,1)S(1)} %get-tuple-element.17), channel_id=1, source_target_pairs={{0,5},{1,6},{2,7},{3,0},{4,1},{5,2},{6,3},{7,4},{8,13},{9,14},{10,... | collective-permute-start | bytes 442376 | tf_op jit(solution)/shard_map/ppermute | solution.py:30
  268.7 9.8 %collective-permute-start.5 = (bf16[1,192,384]{2,1,0:T(8,128)(2,1)S(1)}, bf16[1,192,384]{2,1,0:T(8,128)(2,1)S(1)}, u32[]{:S(2)}, u32[]{:S(2)}) collective-permute-start(bf16[1,192,384]{2,1,0:T(8,128)(2,1)S(1)} %get-tuple-element.16), channel_id=1, source_target_pairs={{0,6},{1,7},{2,0},{3,1},{4,2},{5,3},{6,4},{7,5},{8,14},{9,15},{10,... | collective-permute-start | bytes 442376 | tf_op jit(solution)/shard_map/ppermute | solution.py:30
  269.6 9.0 %collective-permute-start.6 = (bf16[1,192,384]{2,1,0:T(8,128)(2,1)S(1)}, bf16[1,192,384]{2,1,0:T(8,128)(2,1)S(1)}, u32[]{:S(2)}, u32[]{:S(2)}) collective-permute-start(bf16[1,192,384]{2,1,0:T(8,128)(2,1)S(1)} %get-tuple-element.15), channel_id=1, source_target_pairs={{0,7},{1,0},{2,1},{3,2},{4,3},{5,4},{6,5},{7,6},{8,15},{9,8},{10,9... | collective-permute-start | bytes 442376 | tf_op jit(solution)/shard_map/ppermute | solution.py:30
Sparse Core Ops, SparseCore 0:
  88.5 71.3 all-gather.1
  233.3 68.9 reduce-scatter.1
